TPU v7x, 32 devices: a whole 2x2x4 slice. The times are simulated.
32 devices in a mesh: groups: 2 (over x), turn: 16 (over z, y, core).
Axes of the slice: x: 2, y: 2, z: 4, core: 2. Of those that a mesh axis runs over, the one named last changes fastest.
Arguments:
- raw_pulses: bfloat16 [2, 4096, 16384], P(None, ('groups', 'turn')), parts along dimension 1, may hold values from -6 to 6
- chirp_taps: bfloat16 [2, 4096], replicated, may hold values from -0.0625 to 0.0625
- knot_points: float32 [256], P(('groups', 'turn')), parts along dimension 0, may hold values from -5 to 5
- knot_index: int32 [4096], P(('groups', 'turn')), parts along dimension 0, may hold values from 0 to 127, as said below
- spline_param: float32 [4096], P(('groups', 'turn')), parts along dimension 0, may hold values from 0 to 1
- migration: int32 [128], P(('groups', 'turn')), parts along dimension 0, may hold values from 0 to 511
- azimuth_rate: float32 [1024], P(('groups', 'turn')), parts along dimension 0, may hold values from 0.02 to 0.5
Outputs:
- focused_image: float32 [2, 1024, 2048], P(None, ('groups', 'turn')), parts along dimension 1
There are 2 independent parts, one for each index of `groups`. A program takes and returns all parts, laid end to end along the dimension named above; an argument that names none is the same for every part. Nothing has to cross between parts.
Inputs may be any that keep to these rules, and one draw needn't show every extreme that they name: `knot_index`: Nondecreasing; the pulses p with p // 128 = d use knots d * 8 to d * 8 + 7, the first such pulse the lowest and the last such pulse the highest of them.
All inputs are finite; a program needn't handle non-finite values.
Results may differ from a plain program's by a relative error of at most 0.011.
Values may be sent and summed in bfloat16 or wider, within the bound.
A program may use at most 64 MiB of HBM per device.

v0:
```python
import math

import jax
import jax.numpy as jnp
from jax import lax
from jax.sharding import PartitionSpec as P

R_OUTER = 128
R_INNER = 128
BLK = 32


def shifted(x, axis, by):
    size = lax.axis_size(axis)
    pairs = [(i, i + by) for i in range(size) if 0 <= i + by < size]
    return lax.ppermute(x, axis, pairs)


def dft_table(length, sign):
    line = jnp.arange(length, dtype=jnp.int32)
    product = line[:, None] * line[None, :] % length
    angles = product.astype(jnp.float32) * (2.0 * math.pi / length)
    cosine = jnp.cos(angles)
    sine_part = jnp.sin(angles) * sign
    upper = jnp.stack([cosine, -sine_part])
    lower = jnp.stack([sine_part, cosine])
    return jnp.stack([upper, lower]).astype(jnp.bfloat16)


def twiddle(outer, inner, sign):
    outer_line = jnp.arange(outer, dtype=jnp.int32)[:, None]
    inner_line = jnp.arange(inner, dtype=jnp.int32)[None, :]
    product = outer_line * inner_line % (outer * inner)
    angles = product.astype(jnp.float32) * (2.0 * math.pi / (outer * inner))
    return (jnp.cos(angles), jnp.sin(angles) * sign)


def rotate_by(signal, real_part, imag_part):
    return jnp.stack(
        [
            signal[0] * real_part - signal[1] * imag_part,
            signal[0] * imag_part + signal[1] * real_part,
        ]
    )


def along_outer(matrix, signal):
    return jnp.einsum("dcak,cbaj->dbkj", matrix, signal, preferred_element_type=jnp.float32)


def along_inner(matrix, signal):
    return jnp.einsum("dcak,cbia->dbik", matrix, signal, preferred_element_type=jnp.float32)


def make_plan(outer, inner):
    minus_turn = twiddle(outer, inner, -1.0)
    plus_turn = twiddle(outer, inner, 1.0)
    return (
        dft_table(outer, -1.0),
        minus_turn,
        dft_table(inner, -1.0),
        dft_table(inner, 1.0),
        plus_turn,
        dft_table(outer, 1.0),
    )


def forward(signal, plan):
    section = along_outer(plan[0], signal)
    section = rotate_by(section, plan[1][0], plan[1][1]).astype(jnp.bfloat16)
    return along_inner(plan[2], section)


def backward(spectrum, plan, last_matrix):
    section = along_inner(plan[3], spectrum)
    section = rotate_by(section, plan[4][0], plan[4][1]).astype(jnp.bfloat16)
    return along_outer(last_matrix, section)


def spline_weights(position):
    rest = 1.0 - position
    square = position * position
    cube = square * position
    return (
        rest * rest * rest / 6.0,
        (3.0 * cube - 6.0 * square + 4.0) / 6.0,
        (-3.0 * cube + 3.0 * square + 3.0 * position + 1.0) / 6.0,
        cube / 6.0,
    )


def frequency_square(outer, inner):
    total = outer * inner
    freq = (
        jnp.arange(outer, dtype=jnp.int32)[:, None]
        + outer * jnp.arange(inner, dtype=jnp.int32)[None, :]
    )
    centred = jnp.where(freq < total // 2, freq, freq - total)
    return (centred * centred).astype(jnp.float32) / total


def local(raw_pulses, chirp_taps, knot_points, knot_index, spline_param, migration, azimuth_rate):
    turn_count = lax.axis_size("turn")
    pulse_count = raw_pulses.shape[1]
    range_len = raw_pulses.shape[2]
    bin_local = azimuth_rate.shape[0]
    bins_total = bin_local * turn_count
    pulses_total = pulse_count * turn_count
    block_count = pulse_count // BLK
    next_points = shifted(knot_points[:3], "turn", -1)
    extended = jnp.concatenate([knot_points, next_points])
    knot_local = knot_index - lax.axis_index("turn") * knot_points.shape[0]
    slots = jnp.arange(extended.shape[0], dtype=jnp.int32)

    def knot_value(step):
        picked = jnp.where(slots[None, :] == (knot_local + step)[:, None], extended[None, :], 0.0)
        return jnp.sum(picked, axis=1)

    weights = spline_weights(spline_param)
    displace = weights[0] * knot_value(0)
    for step in range(1, 4):
        displace = displace + weights[step] * knot_value(step)
    phase = -4.0 * math.pi * displace
    cos_all = jnp.cos(phase)
    sin_all = jnp.sin(phase)
    range_plan = make_plan(R_OUTER, R_INNER)
    padded = jnp.pad(chirp_taps, ((0, 0), (0, range_len - chirp_taps.shape[1]))).reshape(
        2, 1, R_OUTER, R_INNER
    )
    chirp_spec = forward(padded, range_plan)[:, 0]

    def compress(block_id):
        start = block_id * BLK
        pulse_block = lax.dynamic_slice_in_dim(raw_pulses, start, BLK, 1).reshape(
            2, BLK, R_OUTER, R_INNER
        )
        spectrum = forward(pulse_block, range_plan)
        matched = rotate_by(spectrum, chirp_spec[0][None], -chirp_spec[1][None]).astype(
            jnp.bfloat16
        )
        offset = migration[block_id]
        full = backward(matched, range_plan, range_plan[5]).reshape(2, BLK, range_len) * (
            1.0 / range_len
        )
        window = lax.dynamic_slice_in_dim(full, offset, bins_total, 2)
        cos_block = lax.dynamic_slice_in_dim(cos_all, start, BLK, 0)
        sin_block = lax.dynamic_slice_in_dim(sin_all, start, BLK, 0)
        return rotate_by(window, cos_block[:, None], sin_block[:, None]).astype(jnp.bfloat16)

    stacked = lax.map(compress, jnp.arange(block_count, dtype=jnp.int32))
    pulse_rows = jnp.transpose(stacked, (1, 0, 2, 3)).reshape(2, pulse_count, bins_total)
    moved = lax.all_to_all(pulse_rows, "turn", split_axis=2, concat_axis=1, tiled=True)
    columns = jnp.transpose(moved, (0, 2, 1))
    azimuth_plan = make_plan(turn_count, pulse_count)
    spectrum = forward(columns.reshape(2, bin_local, turn_count, pulse_count), azimuth_plan)
    quad = frequency_square(turn_count, pulse_count)
    angle_map = math.pi * azimuth_rate[:, None, None] * quad[None]
    focused = rotate_by(spectrum, jnp.cos(angle_map), jnp.sin(angle_map)).astype(jnp.bfloat16)
    image = backward(focused, azimuth_plan, azimuth_plan[5]).reshape(2, bin_local, pulses_total)
    return image * (1.0 / pulses_total)


def solution(mesh):
    in_specs = (
        P(None, ("groups", "turn"), None),
        P(),
        P(("groups", "turn")),
        P(("groups", "turn")),
        P(("groups", "turn")),
        P(("groups", "turn")),
        P(("groups", "turn")),
    )
    out_specs = P(None, ("groups", "turn"), None)
    return jax.shard_map(local, mesh=mesh, in_specs=in_specs, out_specs=out_specs, check_vma=False)
```

profile of v0, /device:TPU:0, one launch (start us, length us, event | category | flops | bytes accessed | tf_op | source)
XLA Modules:
  0.0 135.1 jit_solution(18162211956038909518)
XLA Ops:
  0.0 1.4 %collective-permute-start = (f32[3]{0:T(128)}, f32[3]{0:T(128)S(1)}, u32[]{:S(2)}, u32[]{:S(2)}) collective-permute-start(f32[3]{0:T(128)} %bitcast.278), channel_id=1, source_target_pairs={{1,0},{2,1},{3,2},{4,3},{5,4},{6,5},{7,6},{8,7},{9,8},{10,9},{11,1... | collective-permute-start | bytes 44 | tf_op jit(solution)/shard_map/ppermute | solution.py:16
  2.8 0.8 pad_bitcast_fusion
  4.9 0.7 broadcast_add_fusion
  5.9 106.2 %while.14 = (s32[]{:T(128)}, bf16[4,2,32,512]{3,2,0,1:T(8,128)(2,1)S(1)}, s32[4]{0:T(128)S(1)}, bf16[2,128,16384]{2,1,0:T(8,128)(2,1)}, bf16[2,2,128,128]{3,2,1,...) while((s32[]{:T(128)}, ...), condition=%wide.region_5.6_spmd.clone.clone, body=%wide.region_4.5_spmd.clone.clone.sunk | while | flops 2174435328 | bytes 70779976 | solution.py:150
  7.1 1.7 %constant_dynamic-slice_fusion.2 = bf16[2,32,16384]{2,1,0:T(8,128)(2,1)S(1)} fusion(bf16[2,128,16384]{2,1,0:T(8,128)(2,1)} %get-tuple-element.443, s32[]{:T(128)S(6)} %select_n.327), kind=kLoop, calls=%fused_computation.48.clone.1 | loop fusion | bytes 4194308 | tf_op jit(solution)/shard_map/while/body/eval_jaxpr/dynamic_slice | solution.py:134
  9.4 0.8 convolution_bitcast_fusion.10
  10.5 0.6 subtract_convert_fusion.9
  11.1 0.8 convolution_bitcast_fusion.11
  12.5 0.8 convolution_bitcast_fusion.12
  13.5 0.6 subtract_convert_fusion.11
  14.1 2.7 %fusion.134 = f32[2,32,128,128]{2,3,0,1:T(8,128)} fusion(bf16[1,32,128,128]{2,3,0,1:T(8,128)(2,1)S(1)} %get-tuple-element.400, bf16[1,32,128,128]{2,3,0,1:T(8,128)(2,1)S(1)} %get-tuple-element.401, bf16[2,2,128,128]{3,2,1,0:T(8,128)(2,1)S(1)} %get-tuple-element.447), kind=kOutput, calls=%fused_computation.4.clone.1 | convolution fusion | flops 542113792 | bytes 6422528 | tf_op jit(solution)/shard_map/while/body/eval_jaxpr/dcak,cbaj->dbkj/dot_general | solution.py:48
  16.8 5.7 %copy.128 = f32[2,32,128,128]{3,2,1,0:T(8,128)} copy(f32[2,32,128,128]{2,3,0,1:T(8,128)} %fusion.134) | data formatting | bytes 8388608 | tf_op jit(solution)/shard_map/while/body/eval_jaxpr/mul | solution.py:142
  22.4 4.9 %mul.2106 = f32[2,32,16384]{2,1,0:T(8,128)} reshape(f32[2,32,128,128]{3,2,1,0:T(8,128)} %copy.128) | data formatting | bytes 8388608 | tf_op jit(solution)/shard_map/while/body/eval_jaxpr/mul | solution.py:142
  31.4 1.0 fusion.135
  33.6 1.7 %constant_dynamic-slice_fusion.2 = bf16[2,32,16384]{2,1,0:T(8,128)(2,1)S(1)} fusion(bf16[2,128,16384]{2,1,0:T(8,128)(2,1)} %get-tuple-element.443, s32[]{:T(128)S(6)} %select_n.327), kind=kLoop, calls=%fused_computation.48.clone.1 | loop fusion | bytes 4194308 | tf_op jit(solution)/shard_map/while/body/eval_jaxpr/dynamic_slice | solution.py:134
  36.0 0.8 convolution_bitcast_fusion.10
  37.0 0.6 subtract_convert_fusion.9
  37.6 0.8 convolution_bitcast_fusion.11
  39.0 0.8 convolution_bitcast_fusion.12
  40.1 0.6 subtract_convert_fusion.11
  40.7 2.7 %fusion.134 = f32[2,32,128,128]{2,3,0,1:T(8,128)} fusion(bf16[1,32,128,128]{2,3,0,1:T(8,128)(2,1)S(1)} %get-tuple-element.400, bf16[1,32,128,128]{2,3,0,1:T(8,128)(2,1)S(1)} %get-tuple-element.401, bf16[2,2,128,128]{3,2,1,0:T(8,128)(2,1)S(1)} %get-tuple-element.447), kind=kOutput, calls=%fused_computation.4.clone.1 | convolution fusion | flops 542113792 | bytes 6422528 | tf_op jit(solution)/shard_map/while/body/eval_jaxpr/dcak,cbaj->dbkj/dot_general | solution.py:48
  43.3 5.7 %copy.128 = f32[2,32,128,128]{3,2,1,0:T(8,128)} copy(f32[2,32,128,128]{2,3,0,1:T(8,128)} %fusion.134) | data formatting | bytes 8388608 | tf_op jit(solution)/shard_map/while/body/eval_jaxpr/mul | solution.py:142
  49.0 4.9 %mul.2106 = f32[2,32,16384]{2,1,0:T(8,128)} reshape(f32[2,32,128,128]{3,2,1,0:T(8,128)} %copy.128) | data formatting | bytes 8388608 | tf_op jit(solution)/shard_map/while/body/eval_jaxpr/mul | solution.py:142
  58.0 1.0 fusion.135
  60.2 1.7 %constant_dynamic-slice_fusion.2 = bf16[2,32,16384]{2,1,0:T(8,128)(2,1)S(1)} fusion(bf16[2,128,16384]{2,1,0:T(8,128)(2,1)} %get-tuple-element.443, s32[]{:T(128)S(6)} %select_n.327), kind=kLoop, calls=%fused_computation.48.clone.1 | loop fusion | bytes 4194308 | tf_op jit(solution)/shard_map/while/body/eval_jaxpr/dynamic_slice | solution.py:134
  62.5 0.8 convolution_bitcast_fusion.10
  63.6 0.6 subtract_convert_fusion.9
  64.2 0.8 convolution_bitcast_fusion.11
  65.6 0.8 convolution_bitcast_fusion.12
  66.6 0.6 subtract_convert_fusion.11
  67.2 2.7 %fusion.134 = f32[2,32,128,128]{2,3,0,1:T(8,128)} fusion(bf16[1,32,128,128]{2,3,0,1:T(8,128)(2,1)S(1)} %get-tuple-element.400, bf16[1,32,128,128]{2,3,0,1:T(8,128)(2,1)S(1)} %get-tuple-element.401, bf16[2,2,128,128]{3,2,1,0:T(8,128)(2,1)S(1)} %get-tuple-element.447), kind=kOutput, calls=%fused_computation.4.clone.1 | convolution fusion | flops 542113792 | bytes 6422528 | tf_op jit(solution)/shard_map/while/body/eval_jaxpr/dcak,cbaj->dbkj/dot_general | solution.py:48
  69.9 5.7 %copy.128 = f32[2,32,128,128]{3,2,1,0:T(8,128)} copy(f32[2,32,128,128]{2,3,0,1:T(8,128)} %fusion.134) | data formatting | bytes 8388608 | tf_op jit(solution)/shard_map/while/body/eval_jaxpr/mul | solution.py:142
  75.6 4.9 %mul.2106 = f32[2,32,16384]{2,1,0:T(8,128)} reshape(f32[2,32,128,128]{3,2,1,0:T(8,128)} %copy.128) | data formatting | bytes 8388608 | tf_op jit(solution)/shard_map/while/body/eval_jaxpr/mul | solution.py:142
  84.5 1.0 fusion.135
  86.8 1.7 %constant_dynamic-slice_fusion.2 = bf16[2,32,16384]{2,1,0:T(8,128)(2,1)S(1)} fusion(bf16[2,128,16384]{2,1,0:T(8,128)(2,1)} %get-tuple-element.443, s32[]{:T(128)S(6)} %select_n.327), kind=kLoop, calls=%fused_computation.48.clone.1 | loop fusion | bytes 4194308 | tf_op jit(solution)/shard_map/while/body/eval_jaxpr/dynamic_slice | solution.py:134
  89.1 0.8 convolution_bitcast_fusion.10
  90.1 0.6 subtract_convert_fusion.9
  90.8 0.8 convolution_bitcast_fusion.11
  92.1 0.8 convolution_bitcast_fusion.12
  93.8 2.7 %fusion.134 = f32[2,32,128,128]{2,3,0,1:T(8,128)} fusion(bf16[1,32,128,128]{2,3,0,1:T(8,128)(2,1)S(1)} %get-tuple-element.400, bf16[1,32,128,128]{2,3,0,1:T(8,128)(2,1)S(1)} %get-tuple-element.401, bf16[2,2,128,128]{3,2,1,0:T(8,128)(2,1)S(1)} %get-tuple-element.447), kind=kOutput, calls=%fused_computation.4.clone.1 | convolution fusion | flops 542113792 | bytes 6422528 | tf_op jit(solution)/shard_map/while/body/eval_jaxpr/dcak,cbaj->dbkj/dot_general | solution.py:48
  96.4 5.7 %copy.128 = f32[2,32,128,128]{3,2,1,0:T(8,128)} copy(f32[2,32,128,128]{2,3,0,1:T(8,128)} %fusion.134) | data formatting | bytes 8388608 | tf_op jit(solution)/shard_map/while/body/eval_jaxpr/mul | solution.py:142
  102.1 4.9 %mul.2106 = f32[2,32,16384]{2,1,0:T(8,128)} reshape(f32[2,32,128,128]{3,2,1,0:T(8,128)} %copy.128) | data formatting | bytes 8388608 | tf_op jit(solution)/shard_map/while/body/eval_jaxpr/mul | solution.py:142
  111.1 1.0 fusion.135
  112.2 0.9 copy.71
  113.0 8.2 %all-to-all-start = ((bf16[2,128,512]{1,0,2:T(2,128)(2,1)}), bf16[2,128,512]{1,0,2:T(2,128)(2,1)S(1)}, u32[]{:S(2)}, u32[]{:S(2)}) async-start(bf16[2,128,512]{1,0,2:T(2,128)(2,1)} %copy.71), calls=%async_computation | async-start | bytes 524288 | tf_op jit(solution)/shard_map/all_to_all | solution.py:152
  121.3 10.0 %all-to-all-done = bf16[2,128,512]{1,0,2:T(2,128)(2,1)S(1)} async-done(((bf16[2,128,512]{1,0,2:T(2,128)(2,1)}), bf16[2,128,512]{1,0,2:T(2,128)(2,1)S(1)}, u32[]{:S(2)}, u32[]{:S(2)}) %all-to-all-start) | async-done | bytes 262176 | tf_op jit(solution)/shard_map/all_to_all | solution.py:152
  131.9 1.2 fusion.39
  134.0 1.1 copy.75
  (88 shorter events, 17.2 us)
Async XLA Ops:
  0.0 5.6 %copy-start.1 = (f32[8]{0:T(128)S(1)}, f32[8]{0:T(128)}, u32[]{:S(2)}) copy-start(f32[8]{0:T(128)} %param.11) | copy-start | bytes 100
  0.0 5.8 %copy-start = (f32[128]{0:T(128)S(1)}, f32[128]{0:T(128)}, u32[]{:S(2)}) copy-start(f32[128]{0:T(128)} %param.13) | copy-start | bytes 1540
  0.0 5.9 %copy-start.2 = (s32[4]{0:T(128)S(1)}, s32[4]{0:T(128)}, u32[]{:S(2)}) copy-start(s32[4]{0:T(128)} %param.14) | copy-start | bytes 52
  0.0 5.6 %collective-permute-start = (f32[3]{0:T(128)}, f32[3]{0:T(128)S(1)}, u32[]{:S(2)}, u32[]{:S(2)}) collective-permute-start(f32[3]{0:T(128)} %bitcast.278), channel_id=1, source_target_pairs={{1,0},{2,1},{3,2},{4,3},{5,4},{6,5},{7,6},{8,7},{9,8},{10,9},{11,1... | collective-permute-start | bytes 44 | tf_op jit(solution)/shard_map/ppermute | solution.py:16
  5.9 115.3 %copy-start.3 = (f32[32]{0:T(128)S(1)}, f32[32]{0:T(128)}, u32[]{:S(2)}) copy-start(f32[32]{0:T(128)} %param.15) | copy-start | bytes 388
  113.0 18.2 %all-to-all-start = ((bf16[2,128,512]{1,0,2:T(2,128)(2,1)}), bf16[2,128,512]{1,0,2:T(2,128)(2,1)S(1)}, u32[]{:S(2)}, u32[]{:S(2)}) async-start(bf16[2,128,512]{1,0,2:T(2,128)(2,1)} %copy.71), calls=%async_computation | async-start | bytes 524288 | tf_op jit(solution)/shard_map/all_to_all | solution.py:152
where the time goes:
time: 137 us; the launch traced here: 135 us
  local copies, waits for them, and re-layouts  60.1 us (44%)
  matrix products  21.1 us (15%)
  other arithmetic  18.1 us (13%)
  loops' own time  16 us (12%)
  waiting for transfers between devices  9.97 us (7%)
  starting transfers between devices  9.58 us (7%)
    mul x8, local copies, waits for them, and re-layouts, compress(): backward(matched, range_plan, range_plan[5]).reshape(2, BLK, range_len)  42.5 us
    another operation x1, loops' own time, local(): stacked = lax.map(compress, jnp.arange(block_count, dtype=jnp.int32))  16 us
    dot_general x11, matrix products, along_outer(): jnp.einsum('dcak,cbaj->dbkj', matrix, signal, preferred_element_type=jnp....  14.4 us
    another operation x23, other arithmetic  10.1 us
    all_to_all x1, waiting for transfers between devices, local(): lax.all_to_all(pulse_rows, 'turn', split_axis=2, concat_axis=1, tiled=True)  9.97 us
    all_to_all x1, starting transfers between devices, local(): lax.all_to_all(pulse_rows, 'turn', split_axis=2, concat_axis=1, tiled=True)  8.17 us
    dynamic_slice x4, local copies, waits for them, and re-layouts, compress(): lax.dynamic_slice_in_dim(raw_pulses, start, BLK, 1)  6.96 us
    dot_general x11, matrix products, along_inner(): jnp.einsum('dcak,cbia->dbik', matrix, signal, preferred_element_type=jnp....  6.68 us
  transfers between devices with their start and end apart: 2, of which 1 were waited for; matrix products, arithmetic and copies ran while one was open for 3% of the time, Pallas kernels for 0%

commit v1 on v0

v1 whole, which is shorter than its diff:
```python
import functools
import math

import jax
import jax.numpy as jnp
import numpy as np
from jax import lax
from jax.experimental import pallas as pl
from jax.experimental.pallas import tpu as pltpu
from jax.sharding import PartitionSpec as P

BLK = 32
MIGMAX = 512
LANES = 128
F32 = jnp.float32
BF16 = jnp.bfloat16


def table_np(length, sign):
    line = np.arange(length)
    angles = (line[:, None] * line[None, :] % length) * (2.0 * math.pi / length)
    c, s = np.cos(angles), np.sin(angles) * sign
    return np.concatenate(
        [np.concatenate([c, s], 1), np.concatenate([-s, c], 1)], 0
    ).astype(BF16)


def twiddle_np(outer, inner, sign, scale):
    angles = (np.arange(outer)[:, None] * np.arange(inner)[None, :] % (outer * inner)) * (
        2.0 * math.pi / (outer * inner)
    )
    return np.stack([np.cos(angles) * scale, np.sin(angles) * sign * scale]).astype(np.float32)


def transform(values, sign):
    n = len(values)
    if n == 1:
        return values
    even = transform(values[0::2], sign)
    odd = transform(values[1::2], sign)
    low, high = [], []
    for k in range(n // 2):
        (er, ei), (zr, zi) = even[k], odd[k]
        if k == 0:
            tr, ti = zr, zi
        elif 4 * k == n:
            tr, ti = (-zi, zr) if sign > 0 else (zi, -zr)
        elif 8 * k == n:
            h = math.sqrt(0.5)
            tr, ti = ((zr - zi) * h, (zr + zi) * h) if sign > 0 else ((zr + zi) * h, (zi - zr) * h)
        elif 8 * k == 3 * n:
            h = math.sqrt(0.5)
            tr, ti = (
                ((-zr - zi) * h, (zr - zi) * h) if sign > 0 else ((zi - zr) * h, (-zr - zi) * h)
            )
        else:
            c = math.cos(2 * math.pi * k / n)
            s = math.sin(2 * math.pi * k / n) * sign
            tr, ti = zr * c - zi * s, zr * s + zi * c
        low.append((er + tr, ei + ti))
        high.append((er - tr, ei - ti))
    return low + high


def cos_sin_quarters(quarters):
    whole = jnp.floor(quarters + 0.5)
    x = (quarters - whole) * (0.5 * math.pi)
    n = whole.astype(jnp.int32)
    z = x * x
    s = x + x * z * ((-1.9515295891e-4 * z + 8.3321608736e-3) * z - 1.6666654611e-1)
    c = 1.0 - 0.5 * z + z * z * (
        (2.443315711809948e-5 * z - 1.388731625493765e-3) * z + 4.166664568298827e-2
    )
    odd = (n & 1) == 1
    cos = jnp.where(odd, s, c)
    sin = jnp.where(odd, c, s)
    cos = jnp.where(((n + 1) & 2) == 2, -cos, cos)
    sin = jnp.where((n & 2) == 2, -sin, sin)
    return cos, sin


def build_taps(chirp_ref, taps_ref, columns):
    sub = lax.broadcasted_iota(jnp.int32, (LANES, LANES), 0)
    lane = lax.broadcasted_iota(jnp.int32, (LANES, LANES), 1)
    keep = lane >= sub
    for d in range(2):
        before = jnp.zeros((LANES, LANES), F32)
        for block in range(columns + 1):
            if block < columns:
                row = chirp_ref[d : d + 1, block * LANES : (block + 1) * LANES].astype(F32)
                turned = pltpu.roll(
                    jnp.broadcast_to(row, (LANES, LANES)), 0, 1, stride=1, stride_axis=0
                )
            else:
                turned = jnp.zeros((LANES, LANES), F32)
            taps_ref[d * LANES : (d + 1) * LANES, block * LANES : (block + 1) * LANES] = jnp.where(
                keep, turned, before
            ).astype(BF16)
            before = turned


def shift_block(raw_ref, moved_ref, offset, block, columns):
    whole = offset // LANES
    part = offset - whole * LANES
    lane = lax.broadcasted_iota(jnp.int32, (BLK, LANES), 1)
    keep = lane < LANES - part
    turn_by = lax.rem(LANES - part, LANES)
    rows = slice(block * BLK, (block + 1) * BLK)
    for c in range(2):
        before = None
        for j in range(columns + 1):
            start = pl.multiple_of(whole * LANES + j * LANES, LANES)
            piece = raw_ref[c, rows, pl.ds(start, LANES)].astype(F32)
            piece = pltpu.roll(piece, turn_by, 1)
            if before is not None:
                moved_ref[c, rows, (j - 1) * LANES : j * LANES] = jnp.where(
                    keep, before, piece
                ).astype(BF16)
            before = piece


def phases(knot_at, slots, knot_local, position):
    rest = 1.0 - position
    square = position * position
    cube = square * position
    weights = (
        rest * rest * rest / 6.0,
        (3.0 * cube - 6.0 * square + 4.0) / 6.0,
        (-3.0 * cube + 3.0 * square + 3.0 * position + 1.0) / 6.0,
        cube / 6.0,
    )
    displace = jnp.zeros_like(position)
    for step in range(4):
        value = jnp.zeros_like(position)
        for slot in range(slots):
            value = jnp.where(knot_local + step == slot, knot_at(slot), value)
        displace = displace + weights[step] * value
    return cos_sin_quarters(-8.0 * displace)


def compress_bins(taps_ref, moved_ref, start, width, cos, sin):
    samples = jnp.concatenate(
        [moved_ref[0, :, pl.ds(start, width)], moved_ref[1, :, pl.ds(start, width)]], axis=0
    )
    both = lax.dot_general(
        taps_ref[...], samples, (((1,), (1,)), ((), ())), preferred_element_type=F32
    )
    half = both.shape[1] // 2
    real = both[:LANES, :half] + both[LANES:, half:]
    imag = both[:LANES, half:] - both[LANES:, :half]
    return (real * cos - imag * sin).astype(BF16), (real * sin + imag * cos).astype(BF16)


def focus_maps(rate_at, bins, turn_count, inner, cos_ref, sin_ref):
    sub = lax.broadcasted_iota(jnp.int32, (bins, inner), 0)
    rate = jnp.zeros((bins, inner), F32)
    for r in range(bins):
        rate = jnp.where(sub == r, rate_at(r), rate)
    total = turn_count * inner
    lane = lax.broadcasted_iota(jnp.int32, (1, inner), 1)

    def one(k2):
        freq = k2 + turn_count * lane
        centred = jnp.where(freq < total // 2, freq, freq - total)
        quad = (centred * centred).astype(F32) * (2.0 / total)
        cos, sin = cos_sin_quarters(rate * quad)
        at = k2 * bins
        if not isinstance(k2, int):
            at = pl.multiple_of(at, bins)
        cos_ref[pl.ds(at, bins), :] = cos
        sin_ref[pl.ds(at, bins), :] = sin

    if turn_count <= 16:
        for k2 in range(turn_count):
            one(k2)
    else:
        pl.loop(0, turn_count)(one)


def azimuth(inbox_ref, gm_ref, gp_ref, fm_ref, fp_ref, cos_ref, sin_ref, half_ref, spec_ref, out_ref):
    turn_count, _, bins, inner = inbox_ref.shape
    step = 16
    rows = turn_count * bins
    chunk = min(rows, 512)
    for r in range(0, bins, step):
        values = [
            (
                inbox_ref[s, 0, r : r + step, :].astype(F32),
                inbox_ref[s, 1, r : r + step, :].astype(F32),
            )
            for s in range(turn_count)
        ]
        for k2, (re, im) in enumerate(transform(values, -1)):
            if k2:
                gr, gi = gm_ref[0, k2 : k2 + 1, :], gm_ref[1, k2 : k2 + 1, :]
                re, im = re * gr - im * gi, re * gi + im * gr
            at = k2 * bins + r
            half_ref[at : at + step, :inner] = re.astype(BF16)
            half_ref[at : at + step, inner:] = im.astype(BF16)
    for at in range(0, rows, chunk):
        here = slice(at, at + chunk)
        spec = jnp.dot(half_ref[here, :], fm_ref[...], preferred_element_type=F32)
        sr, si = spec[:, :inner], spec[:, inner:]
        cr, ci = cos_ref[here, :], sin_ref[here, :]
        half_ref[here, :inner] = (sr * cr - si * ci).astype(BF16)
        half_ref[here, inner:] = (sr * ci + si * cr).astype(BF16)
    for at in range(0, rows, chunk):
        here = slice(at, at + chunk)
        spec_ref[here, :] = jnp.dot(half_ref[here, :], fp_ref[...], preferred_element_type=F32)
    for r in range(0, bins, step):
        values = []
        for k2 in range(turn_count):
            at = k2 * bins + r
            re, im = spec_ref[at : at + step, :inner], spec_ref[at : at + step, inner:]
            gr, gi = gp_ref[0, k2 : k2 + 1, :], gp_ref[1, k2 : k2 + 1, :]
            values.append((re * gr - im * gi, re * gi + im * gr))
        for n2, (re, im) in enumerate(transform(values, 1)):
            out_ref[0, r : r + step, n2 * inner : (n2 + 1) * inner] = re
            out_ref[1, r : r + step, n2 * inner : (n2 + 1) * inner] = im


def range_kernel(migration, knots, raw, chirp, index, position, out, taps, moved, *, columns, bins_total, bin_local):
    slots = knots.shape[0]
    build_taps(chirp, taps, columns)
    for block in range(raw.shape[1] // BLK):
        shift_block(raw, moved, migration[block], block, moved.shape[2] // LANES)
    cos, sin = phases(lambda j: knots[j], slots, index[...], position[...])
    per = LANES // bin_local
    width = (columns + 1) * LANES

    def one(j):
        re, im = compress_bins(taps, moved, pl.multiple_of(j * LANES, LANES), width, cos, sin)
        for u in range(per):
            out[j * per + u, 0] = re[u * bin_local : (u + 1) * bin_local]
            out[j * per + u, 1] = im[u * bin_local : (u + 1) * bin_local]

    pl.loop(0, bins_total // LANES)(one)


def focus_kernel(rate, inbox, gm, gp, fm, fp, out, cos, sin, half, spec):
    turn_count, _, bins, inner = inbox.shape
    focus_maps(lambda r: rate[r], bins, turn_count, inner, cos, sin)
    azimuth(inbox, gm, gp, fm, fp, cos, sin, half, spec, out)


def local(raw_pulses, chirp_taps, knot_points, knot_index, spline_param, migration, azimuth_rate):
    turn_count = lax.axis_size("turn")
    pulses = raw_pulses.shape[1]
    taps_count = chirp_taps.shape[1]
    bin_local = azimuth_rate.shape[0]
    bins_total = bin_local * turn_count
    columns = taps_count // LANES
    width = bins_total + taps_count
    reach = width + MIGMAX
    pairs = [(i, i - 1) for i in range(1, turn_count)]
    next_points = lax.ppermute(knot_points[:3], "turn", pairs)
    knots = jnp.concatenate([knot_points, next_points])
    knot_local = knot_index - lax.axis_index("turn") * knot_points.shape[0]
    smem = pl.BlockSpec(memory_space=pltpu.SMEM)
    vmem = pl.BlockSpec(memory_space=pltpu.VMEM)
    sent = pl.pallas_call(
        functools.partial(range_kernel, columns=columns, bins_total=bins_total, bin_local=bin_local),
        grid=(1,),
        in_specs=[
            smem,
            smem,
            pl.BlockSpec((2, pulses, reach), lambda i: (0, 0, 0)),
            vmem,
            vmem,
            vmem,
        ],
        out_specs=vmem,
        out_shape=jax.ShapeDtypeStruct((turn_count, 2, bin_local, pulses), BF16),
        scratch_shapes=[
            pltpu.VMEM((2 * LANES, taps_count + LANES), BF16),
            pltpu.VMEM((2, pulses, width), BF16),
        ],
        compiler_params=pltpu.CompilerParams(vmem_limit_bytes=60 * 2**20),
    )(migration, knots, raw_pulses, chirp_taps, knot_local.reshape(1, -1), spline_param.reshape(1, -1))
    inbox = lax.all_to_all(sent, "turn", split_axis=0, concat_axis=0, tiled=True)
    gm = twiddle_np(turn_count, pulses, -1.0, 1.0)
    gp = twiddle_np(turn_count, pulses, 1.0, 1.0 / (turn_count * pulses))
    rows = turn_count * bin_local
    return pl.pallas_call(
        focus_kernel,
        in_specs=[smem] + [vmem] * 5,
        out_specs=vmem,
        out_shape=jax.ShapeDtypeStruct((2, bin_local, turn_count * pulses), F32),
        scratch_shapes=[
            pltpu.VMEM((rows, pulses), F32),
            pltpu.VMEM((rows, pulses), F32),
            pltpu.VMEM((rows, 2 * pulses), BF16),
            pltpu.VMEM((rows, 2 * pulses), F32),
        ],
        compiler_params=pltpu.CompilerParams(vmem_limit_bytes=60 * 2**20),
    )(azimuth_rate, inbox, gm, gp, table_np(pulses, -1.0), table_np(pulses, 1.0))


def solution(mesh):
    in_specs = (
        P(None, ("groups", "turn"), None),
        P(),
        P(("groups", "turn")),
        P(("groups", "turn")),
        P(("groups", "turn")),
        P(("groups", "turn")),
        P(("groups", "turn")),
    )
    out_specs = P(None, ("groups", "turn"), None)
    return jax.shard_map(local, mesh=mesh, in_specs=in_specs, out_specs=out_specs, check_vma=False)
```

time: 137 us -> 33.1 us (0.24); the launches traced: 135 us -> 32.8 us
  local copies, waits for them, and re-layouts: 60.1 us -> 0 us
  matrix products: 21.1 us -> 0 us
  blocking collectives: 0 us -> 18.7 us
  loops' own time: 16 us -> 0 us
  other arithmetic: 18.1 us -> 2.43 us
  Pallas kernels: 0 us -> 9.69 us
  waiting for transfers between devices: 9.97 us -> 0.69 us
  starting transfers between devices: 9.58 us -> 1.28 us
    mul x14 -> x0, local copies, waits for them, and re-layouts: 43.9 us -> none  [the longest x8 42.5 us: compress(): backward(matched, range_plan, range_plan[5]).reshape(2, BLK, range_len)]
    dot_general x22 -> x0, matrix products: 21.1 us -> none  [the longest x11 14.4 us: along_outer(): jnp.einsum('dcak,cbaj->dbkj', matrix, signal, preferred_element_type=jnp....]
    all_to_all x0 -> x1, blocking collectives: none -> 18.7 us  [local(): lax.all_to_all(sent, 'turn', split_axis=0, concat_axis=0, tiled=True)]
    another operation x1 -> x0, loops' own time: 16 us -> none  [local(): stacked = lax.map(compress, jnp.arange(block_count, dtype=jnp.int32))]
    another operation x32 -> x0, other arithmetic: 14.9 us -> none
    dynamic_slice x20 -> x0, local copies, waits for them, and re-layouts: 12.1 us -> none  [the longest x4 6.96 us: compress(): lax.dynamic_slice_in_dim(raw_pulses, start, BLK, 1)]
    all_to_all x1 -> x0, waiting for transfers between devices: 9.97 us -> none  [local(): lax.all_to_all(pulse_rows, 'turn', split_axis=2, concat_axis=1, tiled=True)]
    pallas_call x0 -> x2, Pallas kernels: none -> 9.69 us  [the longest x1 6.95 us: local(): pl.pallas_call(functools.partial(range_kernel, columns=columns, bins_tota...]
  transfers between devices with their start and end apart: 2 -> 1, of which waited for: 1 -> 1; matrix products, arithmetic and copies ran while one was open for 3% -> 4% of each run, Pallas kernels for 0% -> 0%
where the time goes in v1:
time: 33.1 us; the launch traced here: 32.8 us
  blocking collectives  18.7 us (56%)
  Pallas kernels  9.69 us (29%)
  other arithmetic  2.43 us (7%)
  starting transfers between devices  1.28 us (4%)
  waiting for transfers between devices  0.69 us (2%)
    all_to_all x1, blocking collectives, local(): lax.all_to_all(sent, 'turn', split_axis=0, concat_axis=0, tiled=True)  18.7 us
    pallas_call x1, Pallas kernels, local(): pl.pallas_call(functools.partial(range_kernel, columns=columns, bins_tota...  6.95 us
    pallas_call x1, Pallas kernels, local(): pl.pallas_call(focus_kernel, in_specs=[smem] + [vmem] * 5, out_specs=vmem...  2.74 us
    ppermute x1, starting transfers between devices, local(): next_points = lax.ppermute(knot_points[:3], 'turn', pairs)  1.28 us
    concatenate x1, other arithmetic, local(): knots = jnp.concatenate([knot_points, next_points])  1.23 us
    reshape x1, other arithmetic, local(): knot_local.reshape(1, -1)  1.2 us
    ppermute x1, waiting for transfers between devices, local(): next_points = lax.ppermute(knot_points[:3], 'turn', pairs)  0.69 us
  transfers between devices with their start and end apart: 1, of which 1 were waited for; matrix products, arithmetic and copies ran while one was open for 4% of the time, Pallas kernels for 0%

profile of v1, /device:TPU:0, one launch (start us, length us, event | category | flops | bytes accessed | tf_op | source)
XLA Modules:
  0.0 32.8 jit_solution(6898780601069662351)
XLA Ops:
  0.0 1.3 %collective-permute-start = (f32[3]{0:T(128)}, f32[3]{0:T(128)S(1)}, u32[]{:S(2)}, u32[]{:S(2)}) collective-permute-start(f32[3]{0:T(128)} %bitcast.5), channel_id=1, source_target_pairs={{1,0},{2,1},{3,2},{4,3},{5,4},{6,5},{7,6},{8,7},{9,8},{10,9},{11,1... | collective-permute-start | bytes 44 | tf_op jit(solution)/shard_map/ppermute | solution.py:256
  1.3 1.2 %subtract_bitcast_fusion.index = s32[1,128]{1,0:T(1,128)} fusion(s32[128]{0:T(128)} %param.14, s32[]{:T(128)S(6)} %mul.3), kind=kLoop, calls=%fused_computation.1 | loop fusion | flops 128 | bytes 1028 | tf_op jit(solution)/shard_map/reshape | solution.py:279
  2.5 0.7 %collective-permute-done = f32[3]{0:T(128)S(1)} collective-permute-done((f32[3]{0:T(128)}, f32[3]{0:T(128)S(1)}, u32[]{:S(2)}, u32[]{:S(2)}) %collective-permute-start) | collective-permute-done | bytes 44 | tf_op jit(solution)/shard_map/ppermute | solution.py:256
  3.2 1.2 %pad_maximum_fusion.knots = f32[11]{0:T(128)} fusion(f32[3]{0:T(128)S(1)} %collective-permute-done, f32[8]{0:T(128)} %param.13), kind=kLoop, calls=%fused_computation | loop fusion | flops 11 | bytes 88 | tf_op jit(solution)/shard_map/concatenate | solution.py:257
  4.4 7.0 %shard_map.109 = bf16[16,2,32,128]{3,2,1,0:T(8,128)(2,1)} custom-call(s32[4]{0:T(128)} %migration.1, f32[11]{0:T(128)} %pad_maximum_fusion.knots, bf16[2,128,16384]{2,1,0:T(8,128)(2,1)} %raw.1, bf16[2,4096]{1,0:T(2,128)(2,1)} %chirp.1, s32[1,128]{1,0:T(1,128)} %subtract_bitcast_fusion.index, f32[1,128]{1,0:T(1,128)} %bitcast.4), custom_call_target="tpu_custom_call" | custom-call | tf_op jit(solution)/shard_map/pallas_call | solution.py:261
  11.4 18.7 %all_to_all.5.inbox = bf16[16,2,32,128]{3,2,1,0:T(8,128)(2,1)} all-to-all(bf16[16,2,32,128]{3,2,1,0:T(8,128)(2,1)} %shard_map.109), channel_id=1, replica_groups=mesh['groups'=2,'turn'=16] {'turn'}, dimensions={0} | all-to-all | bytes 524288 | tf_op jit(solution)/shard_map/all_to_all | solution.py:280
  30.1 2.7 %shard_map.110 = f32[2,32,2048]{2,1,0:T(8,128)} custom-call(f32[32]{0:T(128)} %rate.1, bf16[16,2,32,128]{3,2,1,0:T(8,128)(2,1)} %all_to_all.5.inbox, f32[2,16,128]{2,1,0:T(8,128)} %constant.14.clone.gm, f32[2,16,128]{2,1,0:T(8,128)} %constant.15.clone.gp, bf16[256,256]{1,0:T(8,128)(2,1)} %constant.16.clone.fm, bf16[256,256]{1,0:T(8,128)(2,1)} %constant.17.clone.fp), custom_call_target="tpu_custom_call" | custom-call | tf_op jit(solution)/shard_map/pallas_call | solution.py:284
Async XLA Ops:
  0.0 3.2 %collective-permute-start = (f32[3]{0:T(128)}, f32[3]{0:T(128)S(1)}, u32[]{:S(2)}, u32[]{:S(2)}) collective-permute-start(f32[3]{0:T(128)} %bitcast.5), channel_id=1, source_target_pairs={{1,0},{2,1},{3,2},{4,3},{5,4},{6,5},{7,6},{8,7},{9,8},{10,9},{11,1... | collective-permute-start | bytes 44 | tf_op jit(solution)/shard_map/ppermute | solution.py:256

commit v2 on v1

--- a/solution.py
+++ b/solution.py
@@ -99,24 +99,23 @@
             before = turned
 
 
-def shift_block(raw_ref, moved_ref, offset, block, columns):
-    whole = offset // LANES
-    part = offset - whole * LANES
-    lane = lax.broadcasted_iota(jnp.int32, (BLK, LANES), 1)
-    keep = lane < LANES - part
-    turn_by = lax.rem(LANES - part, LANES)
-    rows = slice(block * BLK, (block + 1) * BLK)
-    for c in range(2):
-        before = None
-        for j in range(columns + 1):
-            start = pl.multiple_of(whole * LANES + j * LANES, LANES)
-            piece = raw_ref[c, rows, pl.ds(start, LANES)].astype(F32)
-            piece = pltpu.roll(piece, turn_by, 1)
-            if before is not None:
-                moved_ref[c, rows, (j - 1) * LANES : j * LANES] = jnp.where(
-                    keep, before, piece
-                ).astype(BF16)
-            before = piece
+def pick_rows(ref, start, offsets):
+    def chosen(x, bit):
+        return (jnp.broadcast_to(offsets, x.shape) & bit) != 0
+
+    bit = MIGMAX // 2
+    size = LANES + bit
+    low = ref[pl.ds(start, size), :]
+    x = jnp.where(chosen(low, bit), ref[pl.ds(start + bit, size), :], low)
+    while bit > 8:
+        bit //= 2
+        size = LANES + bit
+        low = x[:size]
+        x = jnp.where(chosen(low, bit), x[bit : bit + size], low)
+    while bit > 1:
+        bit //= 2
+        x = jnp.where(chosen(x, bit), pltpu.roll(x, x.shape[0] - bit, 0), x)
+    return x[:LANES]
 
 
 def phases(knot_at, slots, knot_local, position):
@@ -138,17 +137,16 @@
     return cos_sin_quarters(-8.0 * displace)
 
 
-def compress_bins(taps_ref, moved_ref, start, width, cos, sin):
-    samples = jnp.concatenate(
-        [moved_ref[0, :, pl.ds(start, width)], moved_ref[1, :, pl.ds(start, width)]], axis=0
-    )
+def compress_block(taps_ref, raw_ref, block, width, real_ref, imag_ref):
+    here = pl.ds(pl.multiple_of(block * LANES, LANES), width)
+    samples = jnp.concatenate([raw_ref[0, :, here], raw_ref[1, :, here]], axis=0)
     both = lax.dot_general(
         taps_ref[...], samples, (((1,), (1,)), ((), ())), preferred_element_type=F32
     )
     half = both.shape[1] // 2
-    real = both[:LANES, :half] + both[LANES:, half:]
-    imag = both[:LANES, half:] - both[LANES:, :half]
-    return (real * cos - imag * sin).astype(BF16), (real * sin + imag * cos).astype(BF16)
+    rows = pl.ds(pl.multiple_of(block * LANES, LANES), LANES)
+    real_ref[rows, :] = both[:LANES, :half] + both[LANES:, half:]
+    imag_ref[rows, :] = both[:LANES, half:] - both[LANES:, :half]
 
 
 def focus_maps(rate_at, bins, turn_count, inner, cos_ref, sin_ref):
@@ -219,28 +217,138 @@
             out_ref[1, r : r + step, n2 * inner : (n2 + 1) * inner] = im
 
 
-def range_kernel(migration, knots, raw, chirp, index, position, out, taps, moved, *, columns, bins_total, bin_local):
-    slots = knots.shape[0]
+def kernel(
+    migration, knots, rate, chirp, index, position, raw_hbm, gm_hbm, gp_hbm, fm_hbm, fp_hbm,
+    out,
+    raw, gm, gp, fm, fp, taps, real, imag, own_knots, next_knots, outbox, inbox, cos_map, sin_map, half, spec,
+    load_sem, knot_sem, send_sem, recv_sem, self_sem,
+):
+    turn_count, _, bin_local, pulses = inbox.shape
+    knot_count = knots.shape[0]
+    per = LANES // bin_local
+    blocks = turn_count // per
+    columns = chirp.shape[1] // LANES
+    me = lax.axis_index("turn")
+    mine, lane_of_me = lax.div(me, per), lax.rem(me, per)
+    mesh_id = pl.DeviceIdType.MESH
+    loads = [
+        pltpu.make_async_copy(src, dst, load_sem.at[i])
+        for i, (src, dst) in enumerate(
+            [
+                (raw_hbm.at[:, :, pl.ds(0, raw.shape[2])], raw),
+                (gm_hbm, gm),
+                (gp_hbm, gp),
+                (fm_hbm, fm),
+                (fp_hbm, fp),
+            ]
+        )
+    ]
+    for load in loads:
+        load.start()
+    barrier = pltpu.get_barrier_semaphore()
+
+    def greet(off):
+        pl.semaphore_signal(
+            barrier, inc=1, device_id={"turn": lax.rem(me + off, turn_count)}, device_id_type=mesh_id
+        )
+
+    if turn_count <= 16:
+        for off in range(1, turn_count):
+            greet(off)
+    else:
+        pl.loop(1, turn_count)(greet)
+    for j in range(min(knot_count, 8)):
+        own_knots[j : j + 1, :] = jnp.full((1, LANES), knots[j], F32)
     build_taps(chirp, taps, columns)
-    for block in range(raw.shape[1] // BLK):
-        shift_block(raw, moved, migration[block], block, moved.shape[2] // LANES)
-    cos, sin = phases(lambda j: knots[j], slots, index[...], position[...])
-    per = LANES // bin_local
+    pl.semaphore_wait(barrier, turn_count - 1)
+    knot_copy = pltpu.make_async_remote_copy(
+        src_ref=own_knots,
+        dst_ref=next_knots,
+        send_sem=knot_sem.at[0],
+        recv_sem=knot_sem.at[1],
+        device_id={"turn": lax.rem(me + turn_count - 1, turn_count)},
+        device_id_type=mesh_id,
+    )
+    knot_copy.start()
+    loads[0].wait()
     width = (columns + 1) * LANES
-
-    def one(j):
-        re, im = compress_bins(taps, moved, pl.multiple_of(j * LANES, LANES), width, cos, sin)
+    extra = MIGMAX // LANES
+    upward = mine >= blocks // 2
+
+    def compress(i):
+        block = jnp.where(upward, i, blocks + extra - 1 - i)
+        compress_block(taps, raw, block, width, real, imag)
+
+    for i in range(extra):
+        compress(i)
+    knot_copy.wait()
+    past = jnp.where(me == turn_count - 1, 0.0, 1.0).astype(F32)
+
+    def knot_at(slot):
+        if slot < knot_count:
+            return knots[slot]
+        return next_knots[slot - knot_count : slot - knot_count + 1, :] * past
+
+    cos, sin = phases(knot_at, knot_count + 3, index[...] - me * knot_count, position[...])
+    pulse = lax.broadcasted_iota(jnp.int32, (1, pulses), 1)
+    offsets = jnp.zeros((1, pulses), jnp.int32)
+    for block in range(pulses // BLK):
+        offsets = jnp.where(pulse // BLK == block, migration[block], offsets)
+
+    def message(peer, sender):
+        return pltpu.make_async_remote_copy(
+            src_ref=outbox.at[peer],
+            dst_ref=inbox.at[sender],
+            send_sem=send_sem.at[peer],
+            recv_sem=recv_sem.at[sender],
+            device_id={"turn": peer},
+            device_id_type=mesh_id,
+        )
+
+    keep = pltpu.make_async_copy(outbox.at[me], inbox.at[me], self_sem)
+
+    def step(k):
+        compress(extra + k)
+        j = jnp.where(upward, k, blocks - 1 - k)
+        start = pl.multiple_of(j * LANES, LANES)
+        yr, yi = pick_rows(real, start, offsets), pick_rows(imag, start, offsets)
+        re = (yr * cos - yi * sin).astype(BF16)
+        im = (yr * sin + yi * cos).astype(BF16)
         for u in range(per):
-            out[j * per + u, 0] = re[u * bin_local : (u + 1) * bin_local]
-            out[j * per + u, 1] = im[u * bin_local : (u + 1) * bin_local]
-
-    pl.loop(0, bins_total // LANES)(one)
-
-
-def focus_kernel(rate, inbox, gm, gp, fm, fp, out, cos, sin, half, spec):
-    turn_count, _, bins, inner = inbox.shape
-    focus_maps(lambda r: rate[r], bins, turn_count, inner, cos, sin)
-    azimuth(inbox, gm, gp, fm, fp, cos, sin, half, spec, out)
+            outbox[j * per + u, 0] = re[u * bin_local : (u + 1) * bin_local]
+            outbox[j * per + u, 1] = im[u * bin_local : (u + 1) * bin_local]
+        for v in range(per):
+            peer = j * per + lax.rem(lane_of_me + v, per)
+
+            @pl.when(peer != me)
+            def _():
+                message(peer, me).start()
+
+        @pl.when(j == mine)
+        def _():
+            keep.start()
+
+    if blocks <= 4:
+        for k in range(blocks):
+            step(k)
+    else:
+        pl.loop(0, blocks)(step)
+
+    focus_maps(lambda r: rate[r], bin_local, turn_count, pulses, cos_map, sin_map)
+    for load in loads[1:]:
+        load.wait()
+    keep.wait()
+
+    def others(body):
+        if turn_count <= 16:
+            for off in range(1, turn_count):
+                body(lax.rem(me + off, turn_count))
+        else:
+            pl.loop(1, turn_count)(lambda off: body(lax.rem(me + off, turn_count)))
+
+    others(lambda peer: message(me, peer).wait_recv())
+    azimuth(inbox, gm, gp, fm, fp, cos_map, sin_map, half, spec, out)
+    others(lambda peer: message(peer, me).wait_send())
 
 
 def local(raw_pulses, chirp_taps, knot_points, knot_index, spline_param, migration, azimuth_rate):
@@ -248,52 +356,60 @@
     pulses = raw_pulses.shape[1]
     taps_count = chirp_taps.shape[1]
     bin_local = azimuth_rate.shape[0]
-    bins_total = bin_local * turn_count
-    columns = taps_count // LANES
-    width = bins_total + taps_count
-    reach = width + MIGMAX
-    pairs = [(i, i - 1) for i in range(1, turn_count)]
-    next_points = lax.ppermute(knot_points[:3], "turn", pairs)
-    knots = jnp.concatenate([knot_points, next_points])
-    knot_local = knot_index - lax.axis_index("turn") * knot_points.shape[0]
+    width = bin_local * turn_count + taps_count
     smem = pl.BlockSpec(memory_space=pltpu.SMEM)
     vmem = pl.BlockSpec(memory_space=pltpu.VMEM)
-    sent = pl.pallas_call(
-        functools.partial(range_kernel, columns=columns, bins_total=bins_total, bin_local=bin_local),
-        grid=(1,),
-        in_specs=[
-            smem,
-            smem,
-            pl.BlockSpec((2, pulses, reach), lambda i: (0, 0, 0)),
-            vmem,
-            vmem,
-            vmem,
-        ],
-        out_specs=vmem,
-        out_shape=jax.ShapeDtypeStruct((turn_count, 2, bin_local, pulses), BF16),
-        scratch_shapes=[
-            pltpu.VMEM((2 * LANES, taps_count + LANES), BF16),
-            pltpu.VMEM((2, pulses, width), BF16),
-        ],
-        compiler_params=pltpu.CompilerParams(vmem_limit_bytes=60 * 2**20),
-    )(migration, knots, raw_pulses, chirp_taps, knot_local.reshape(1, -1), spline_param.reshape(1, -1))
-    inbox = lax.all_to_all(sent, "turn", split_axis=0, concat_axis=0, tiled=True)
+    hbm = pl.BlockSpec(memory_space=pl.ANY)
     gm = twiddle_np(turn_count, pulses, -1.0, 1.0)
     gp = twiddle_np(turn_count, pulses, 1.0, 1.0 / (turn_count * pulses))
     rows = turn_count * bin_local
+    table = pltpu.VMEM((2 * pulses, 2 * pulses), BF16)
+    turns = pltpu.VMEM((2, turn_count, pulses), F32)
+    box = pltpu.VMEM((turn_count, 2, bin_local, pulses), BF16)
     return pl.pallas_call(
-        focus_kernel,
-        in_specs=[smem] + [vmem] * 5,
+        kernel,
+        in_specs=[smem] * 3 + [vmem] * 3 + [hbm] * 5,
         out_specs=vmem,
         out_shape=jax.ShapeDtypeStruct((2, bin_local, turn_count * pulses), F32),
         scratch_shapes=[
+            pltpu.VMEM((2, pulses, width + MIGMAX), BF16),
+            turns,
+            turns,
+            table,
+            table,
+            pltpu.VMEM((2 * LANES, taps_count + LANES), BF16),
+            pltpu.VMEM((width - taps_count + MIGMAX, pulses), F32),
+            pltpu.VMEM((width - taps_count + MIGMAX, pulses), F32),
+            pltpu.VMEM((8, LANES), F32),
+            pltpu.VMEM((8, LANES), F32),
+            box,
+            box,
             pltpu.VMEM((rows, pulses), F32),
             pltpu.VMEM((rows, pulses), F32),
             pltpu.VMEM((rows, 2 * pulses), BF16),
             pltpu.VMEM((rows, 2 * pulses), F32),
+            pltpu.SemaphoreType.DMA((5,)),
+            pltpu.SemaphoreType.DMA((2,)),
+            pltpu.SemaphoreType.DMA((turn_count,)),
+            pltpu.SemaphoreType.DMA((turn_count,)),
+            pltpu.SemaphoreType.DMA,
         ],
-        compiler_params=pltpu.CompilerParams(vmem_limit_bytes=60 * 2**20),
-    )(azimuth_rate, inbox, gm, gp, table_np(pulses, -1.0), table_np(pulses, 1.0))
+        compiler_params=pltpu.CompilerParams(
+            collective_id=0, has_side_effects=True, vmem_limit_bytes=60 * 2**20
+        ),
+    )(
+        migration,
+        knot_points,
+        azimuth_rate,
+        chirp_taps,
+        knot_index.reshape(1, -1),
+        spline_param.reshape(1, -1),
+        raw_pulses,
+        gm,
+        gp,
+        table_np(pulses, -1.0),
+        table_np(pulses, 1.0),
+    )
 
 
 def solution(mesh):

time: 33.1 us -> 22.2 us (0.67)
  blocking collectives: 18.7 us -> 0 us
  Pallas kernels: 9.69 us -> 20.1 us
  other arithmetic: 2.43 us -> 0 us
  local copies, waits for them, and re-layouts: 0 us -> 1.87 us
  starting transfers between devices: 1.28 us -> 0 us
  waiting for transfers between devices: 0.69 us -> 0 us
    all_to_all x1 -> x0, blocking collectives: 18.7 us -> none  [local(): lax.all_to_all(sent, 'turn', split_axis=0, concat_axis=0, tiled=True)]
    pallas_call x2 -> x1, Pallas kernels: 9.69 us -> 20.1 us  [local(): pl.pallas_call(kernel, in_specs=[smem] * 3 + [vmem] * 3 + [hbm] * 5, out_...]
    unnamed x0 -> x1, local copies, waits for them, and re-layouts: none -> 1.87 us
    ppermute x1 -> x0, starting transfers between devices: 1.28 us -> none  [local(): next_points = lax.ppermute(knot_points[:3], 'turn', pairs)]
    concatenate x1 -> x0, other arithmetic: 1.23 us -> none  [local(): knots = jnp.concatenate([knot_points, next_points])]
    reshape x1 -> x0, other arithmetic: 1.2 us -> none  [local(): knot_local.reshape(1, -1)]
    ppermute x1 -> x0, waiting for transfers between devices: 0.69 us -> none  [local(): next_points = lax.ppermute(knot_points[:3], 'turn', pairs)]
  transfers between devices with their start and end apart: 1 -> 0, of which waited for: 1 -> 0; matrix products, arithmetic and copies ran while one was open for 4% -> 0% of each run, Pallas kernels for 0% -> 0%
where the time goes in v2:
time: 22.2 us; the launch traced here: 22 us
  Pallas kernels  20.1 us (91%)
  local copies, waits for them, and re-layouts  1.87 us (8%)
    pallas_call x1, Pallas kernels, local(): pl.pallas_call(kernel, in_specs=[smem] * 3 + [vmem] * 3 + [hbm] * 5, out_...  20.1 us
    unnamed x1, local copies, waits for them, and re-layouts  1.87 us

profile of v2, /device:TPU:0, one launch (start us, length us, event | category | flops | bytes accessed | tf_op | source)
XLA Modules:
  0.0 22.0 jit_solution(13709239993189506055)
XLA Ops:
  0.0 20.1 %shard_map.109 = f32[2,32,2048]{2,1,0:T(8,128)} custom-call(s32[4]{0:T(128)} %migration.1, f32[8]{0:T(128)} %knots.1, f32[32]{0:T(128)} %rate.1, bf16[2,4096]{1,0:T(2,128)(2,1)} %chirp.1, s32[1,128]{1,0:T(1,128)} %bitcast.2, f32[1,128]{1,0:T(1,128)} %bitcast.3, bf16[2,128,16384]{2,1,0:T(8,128)(2,1)} %raw_hbm.1, f32[2,16,128]{2,1,0:T(8,128)} %constant.8.clone.gm_hbm, ...), custom_call_target="tpu_custom_call" | custom-call | tf_op jit(solution)/shard_map/pallas_call | solution.py:369
  20.2 1.9 %copy.13 = f32[2,32,2048]{2,1,0:T(8,128)} copy(f32[2,32,2048]{2,1,0:T(8,128)} %shard_map.109) | data formatting | bytes 1048576

commit v3 on v2

--- a/solution.py
+++ b/solution.py
@@ -137,16 +137,22 @@
     return cos_sin_quarters(-8.0 * displace)
 
 
-def compress_block(taps_ref, raw_ref, block, width, real_ref, imag_ref):
-    here = pl.ds(pl.multiple_of(block * LANES, LANES), width)
-    samples = jnp.concatenate([raw_ref[0, :, here], raw_ref[1, :, here]], axis=0)
+def compress_blocks(taps_ref, raw_ref, first, count, width, real_ref, imag_ref):
+    starts = [(first + b) * LANES for b in range(count)]
+    if not isinstance(first, int):
+        starts = [pl.multiple_of(start, LANES) for start in starts]
+    samples = jnp.concatenate(
+        [raw_ref[c, :, pl.ds(start, width)] for start in starts for c in range(2)], axis=0
+    )
     both = lax.dot_general(
-        taps_ref[...], samples, (((1,), (1,)), ((), ())), preferred_element_type=F32
-    )
-    half = both.shape[1] // 2
-    rows = pl.ds(pl.multiple_of(block * LANES, LANES), LANES)
-    real_ref[rows, :] = both[:LANES, :half] + both[LANES:, half:]
-    imag_ref[rows, :] = both[:LANES, half:] - both[LANES:, :half]
+        samples, taps_ref[...], (((1,), (1,)), ((), ())), preferred_element_type=F32
+    )
+    pulses = raw_ref.shape[1]
+    for b, start in enumerate(starts):
+        xr = both[2 * b * pulses : (2 * b + 1) * pulses]
+        xi = both[(2 * b + 1) * pulses : (2 * b + 2) * pulses]
+        real_ref[pl.ds(start, LANES), :] = (xr[:, :LANES] + xi[:, LANES:]).T
+        imag_ref[pl.ds(start, LANES), :] = (xi[:, :LANES] - xr[:, LANES:]).T
 
 
 def focus_maps(rate_at, bins, turn_count, inner, cos_ref, sin_ref):
@@ -260,6 +266,35 @@
     for j in range(min(knot_count, 8)):
         own_knots[j : j + 1, :] = jnp.full((1, LANES), knots[j], F32)
     build_taps(chirp, taps, columns)
+    width = (columns + 1) * LANES
+    extra = MIGMAX // LANES
+    loads[0].wait()
+    group = 8 if (blocks + extra) % 8 == 0 else 4
+
+    def compress(i):
+        compress_blocks(taps, raw, i * group, group, width, real, imag)
+
+    if blocks + extra == group:
+        compress(0)
+    else:
+        pl.loop(0, (blocks + extra) // group)(compress)
+    pulse = lax.broadcasted_iota(jnp.int32, (1, pulses), 1)
+    offsets = jnp.zeros((1, pulses), jnp.int32)
+    for block in range(pulses // BLK):
+        offsets = jnp.where(pulse // BLK == block, migration[block], offsets)
+
+    def pick(j):
+        start = j * LANES
+        if not isinstance(j, int):
+            start = pl.multiple_of(start, LANES)
+        real[pl.ds(start, LANES), :] = pick_rows(real, start, offsets)
+        imag[pl.ds(start, LANES), :] = pick_rows(imag, start, offsets)
+
+    if blocks <= 4:
+        for j in range(blocks):
+            pick(j)
+    else:
+        pl.loop(0, blocks)(pick)
     pl.semaphore_wait(barrier, turn_count - 1)
     knot_copy = pltpu.make_async_remote_copy(
         src_ref=own_knots,
@@ -270,17 +305,7 @@
         device_id_type=mesh_id,
     )
     knot_copy.start()
-    loads[0].wait()
-    width = (columns + 1) * LANES
-    extra = MIGMAX // LANES
     upward = mine >= blocks // 2
-
-    def compress(i):
-        block = jnp.where(upward, i, blocks + extra - 1 - i)
-        compress_block(taps, raw, block, width, real, imag)
-
-    for i in range(extra):
-        compress(i)
     knot_copy.wait()
     past = jnp.where(me == turn_count - 1, 0.0, 1.0).astype(F32)
 
@@ -290,11 +315,6 @@
         return next_knots[slot - knot_count : slot - knot_count + 1, :] * past
 
     cos, sin = phases(knot_at, knot_count + 3, index[...] - me * knot_count, position[...])
-    pulse = lax.broadcasted_iota(jnp.int32, (1, pulses), 1)
-    offsets = jnp.zeros((1, pulses), jnp.int32)
-    for block in range(pulses // BLK):
-        offsets = jnp.where(pulse // BLK == block, migration[block], offsets)
-
     def message(peer, sender):
         return pltpu.make_async_remote_copy(
             src_ref=outbox.at[peer],
@@ -308,10 +328,9 @@
     keep = pltpu.make_async_copy(outbox.at[me], inbox.at[me], self_sem)
 
     def step(k):
-        compress(extra + k)
         j = jnp.where(upward, k, blocks - 1 - k)
         start = pl.multiple_of(j * LANES, LANES)
-        yr, yi = pick_rows(real, start, offsets), pick_rows(imag, start, offsets)
+        yr, yi = real[pl.ds(start, LANES), :], imag[pl.ds(start, LANES), :]
         re = (yr * cos - yi * sin).astype(BF16)
         im = (yr * sin + yi * cos).astype(BF16)
         for u in range(per):

time: 22.2 us -> 23.6 us (1.063)
  Pallas kernels: 20.1 us -> 21.5 us
    pallas_call x1, Pallas kernels: 20.1 us -> 21.5 us  [local(): pl.pallas_call(kernel, in_specs=[smem] * 3 + [vmem] * 3 + [hbm] * 5, out_...]
where the time goes in v3:
time: 23.6 us; the launch traced here: 23.4 us
  Pallas kernels  21.5 us (91%)
  local copies, waits for them, and re-layouts  1.87 us (8%)
    pallas_call x1, Pallas kernels, local(): pl.pallas_call(kernel, in_specs=[smem] * 3 + [vmem] * 3 + [hbm] * 5, out_...  21.5 us
    unnamed x1, local copies, waits for them, and re-layouts  1.87 us

profile of v3, /device:TPU:0, one launch (start us, length us, event | category | flops | bytes accessed | tf_op | source)
XLA Modules:
  0.0 23.4 jit_solution(17458208061306443116)
XLA Ops:
  0.0 21.5 %shard_map.109 = f32[2,32,2048]{2,1,0:T(8,128)} custom-call(s32[4]{0:T(128)} %migration.1, f32[8]{0:T(128)} %knots.1, f32[32]{0:T(128)} %rate.1, bf16[2,4096]{1,0:T(2,128)(2,1)} %chirp.1, s32[1,128]{1,0:T(1,128)} %bitcast.2, f32[1,128]{1,0:T(1,128)} %bitcast.3, bf16[2,128,16384]{2,1,0:T(8,128)(2,1)} %raw_hbm.1, f32[2,16,128]{2,1,0:T(8,128)} %constant.8.clone.gm_hbm, ...), custom_call_target="tpu_custom_call" | custom-call | tf_op jit(solution)/shard_map/pallas_call | solution.py:388
  21.5 1.9 %copy.13 = f32[2,32,2048]{2,1,0:T(8,128)} copy(f32[2,32,2048]{2,1,0:T(8,128)} %shard_map.109) | data formatting | bytes 1048576
